TPU v7x, 256 devices: a whole 4x4x8 slice. The times are simulated.
256 devices in a mesh: wide: 32 (over x, y, core), narrow: 8 (over z).
Axes of the slice: x: 4, y: 4, z: 8, core: 2. Of those that a mesh axis runs over, the one named last changes fastest.
Arguments:
- blocks: bfloat16 [32, 8, 16, 64, 4096], P('wide', 'narrow'), may hold values from -16 to 16
- row_tile: int32 [32, 8, 16], P('wide', 'narrow'), may hold values from 0 to 15
- col_tile: int32 [32, 8, 16], P('wide', 'narrow'), may hold values from 0 to 63, as said below
- depth_tile: int32 [32, 8, 16], P('wide', 'narrow'), may hold values from 0 to 15
- block_count: int32 [32, 8], P('wide', 'narrow'), may hold values from 4 to 16, as said below
- factor_b: bfloat16 [32768, 256], P(('wide', 'narrow')), may hold values from -40 to 40
- factor_c: bfloat16 [1024, 256], replicated, may hold values from -0.076293945 to 0.076293945
Outputs:
- a_new: float32 [32768, 256], P(('wide', 'narrow'))
- b_new: float32 [32768, 256], P(('wide', 'narrow'))
Inputs may be any that keep to these rules, and one draw needn't show every extreme that they name: `block_count`: every device holds at least 4 live blocks, and some device exactly 16. col_tile // 2 is the index of wide that holds the block's mode-2 factor rows; among the 16 slots of one device, live or not, each such index appears at most 1 times, and some index exactly 1 times.
All inputs are finite; a program needn't handle non-finite values.
Results may differ from a plain program's by a relative error of at most 0.02.
Values may be sent and summed in bfloat16 or wider, within the bound.
No kernel may reach another device: no remote copies, remote signals or barrier semaphores. Data moves between devices by JAX's collectives and lax.ppermute only.
A program may use at most 128 MiB of HBM per device.

v0:
```python
import jax
import jax.numpy as jnp
from jax import lax
from jax.sharding import PartitionSpec as P

TI_DEV = 2


def right_solve(target, matrix):
    chol_lower = jnp.linalg.cholesky(matrix)
    middle = lax.linalg.triangular_solve(
        chol_lower, target, left_side=False, lower=True, transpose_a=True
    )
    return lax.linalg.triangular_solve(
        chol_lower, middle, left_side=False, lower=True, transpose_a=False
    )


def column_gram(matrix):
    return lax.dot_general(
        matrix, matrix, (((0,), (0,)), ((), ())), preferred_element_type=jnp.float32
    )


def depth_mix(one_block, depth_id, factor_c, tile_rows):
    depth_rows = lax.dynamic_slice_in_dim(factor_c, depth_id * tile_rows, tile_rows, 0)
    depth_mixed = lax.dot_general(
        one_block, depth_rows, (((0,), (0,)), ((), ())), preferred_element_type=jnp.float32
    )
    return depth_mixed.reshape(tile_rows, tile_rows, depth_rows.shape[1])


def local(blocks, row_tile, col_tile, depth_tile, block_count, factor_b, factor_c):
    local_blocks = blocks[0, 0]
    first_ids = row_tile[0, 0]
    second_ids = col_tile[0, 0]
    depth_ids = depth_tile[0, 0]
    live_count = block_count[0, 0]
    tile_rows = local_blocks.shape[1]
    rank_width = factor_c.shape[1]
    wide_count = lax.axis_size("wide")
    narrow_count = lax.axis_size("narrow")
    second_local = factor_b.shape[0] // tile_rows
    owners = second_ids // second_local
    inside = second_ids % second_local
    gram_c = column_gram(factor_c)
    gram_b = lax.psum(column_gram(factor_b), ("wide", "narrow"))
    gathered = lax.all_gather(factor_b, "wide", axis=0, tiled=True)
    b_tiles = gathered.reshape(wide_count * second_local, tile_rows, rank_width)
    b_pick = owners * second_local + inside

    def first_step(slot_index, partial_sum):
        one_block = lax.dynamic_index_in_dim(local_blocks, slot_index, 0, False)
        depth_mixed = depth_mix(one_block, depth_ids[slot_index], factor_c, tile_rows)
        b_rows = lax.dynamic_index_in_dim(b_tiles, b_pick[slot_index], 0, False).astype(jnp.float32)
        b_term = jnp.sum(depth_mixed * b_rows[None, :, :], axis=1)
        target = first_ids[slot_index]
        current = lax.dynamic_index_in_dim(partial_sum, target, 0, False)
        return lax.dynamic_update_index_in_dim(partial_sum, current + b_term, target, 0)

    first_part = lax.fori_loop(
        0,
        live_count,
        first_step,
        jnp.zeros((narrow_count * TI_DEV, tile_rows, rank_width), jnp.float32),
    )
    mttkrp_a = lax.psum_scatter(
        first_part.reshape(-1, rank_width), "narrow", scatter_dimension=0, tiled=True
    )
    a_new = right_solve(mttkrp_a, gram_b * gram_c)
    a_half = a_new.astype(jnp.bfloat16)
    a_rows = lax.all_gather(a_half, "narrow", axis=0, tiled=True)
    gram_a = lax.psum(column_gram(a_half), ("wide", "narrow"))
    a_tiles = a_rows.reshape(a_rows.shape[0] // tile_rows, tile_rows, rank_width)
    width_slots = wide_count * second_local
    second_pick = owners * second_local + inside

    def second_step(slot_index, partial_sum):
        one_block = lax.dynamic_index_in_dim(local_blocks, slot_index, 0, False)
        depth_mixed = depth_mix(one_block, depth_ids[slot_index], factor_c, tile_rows)
        a_part = lax.dynamic_index_in_dim(a_tiles, first_ids[slot_index], 0, False).astype(
            jnp.float32
        )
        a_term = jnp.sum(depth_mixed * a_part[:, None, :], axis=0)
        target = second_pick[slot_index]
        current = lax.dynamic_index_in_dim(partial_sum, target, 0, False)
        return lax.dynamic_update_index_in_dim(partial_sum, current + a_term, target, 0)

    second_part = lax.fori_loop(
        0, live_count, second_step, jnp.zeros((width_slots, tile_rows, rank_width), jnp.float32)
    )
    mttkrp_b = lax.psum_scatter(
        second_part.reshape(-1, rank_width), "wide", scatter_dimension=0, tiled=True
    )
    b_new = right_solve(mttkrp_b, gram_a * gram_c)
    return (a_new, b_new)


def solution(mesh):
    return jax.shard_map(
        local,
        mesh=mesh,
        in_specs=(
            P("wide", "narrow", None, None, None),
            P("wide", "narrow", None),
            P("wide", "narrow", None),
            P("wide", "narrow", None),
            P("wide", "narrow"),
            P(("wide", "narrow"), None),
            P(),
        ),
        out_specs=(P(("wide", "narrow"), None), P(("wide", "narrow"), None)),
        check_vma=False,
    )
```

profile of v0, /device:TPU:2, one launch (start us, length us, event | category | flops | bytes accessed | tf_op | source)
XLA Modules:
  0.0 688.1 jit_solution(2137662635349681206)
XLA Ops:
  8.8 1.8 fusion.35
  10.8 15.6 %copy.22 = bf16[1,1,16,64,4096]{3,4,2,1,0:T(8,128)(2,1)} copy(bf16[1,1,16,64,4096]{4,3,2,1,0:T(8,128)(2,1)} %param.16) | data formatting | bytes 16777216 | tf_op args[0]
  26.4 36.2 %all-gather.2.cloned.1.call-done = bf16[4096,256]{1,0:T(8,128)(2,1)} async-done(((bf16[128,256]{1,0:T(8,128)(2,1)}), bf16[4096,256]{1,0:T(8,128)(2,1)}) %all-gather.2.cloned.1.call-update) | async-done | bytes 2097168 | tf_op jit(solution)/shard_map/all_gather | solution.py:48
  62.7 144.2 %while.28 = (s32[]{:T(128)}, f32[16,64,256]{2,1,0:T(8,128)S(1)}, s32[]{:T(128)}, s32[16]{0:T(128)S(1)}, bf16[16,64,4096]{1,2,0:T(8,128)(2,1)}, /*index=5*/s32[16...) while((s32[]{:T(128)}, f32[16,64,256]{2,1,0:T(8,128)S(1)}, ...), condition=%wide.region_7.9_spmd, body=%wide.region_5.8_spmd.sunk | while | flops 136331280 | bytes 2556253 | solution.py:61
  207.9 64.7 %all-reduce.4.cloned.1.call-done = f32[256,256]{0,1:T(8,128)} async-done(((f32[256,256]{0,1:T(8,128)}), f32[256,256]{0,1:T(8,128)}) %all-reduce.4.cloned.1.call-update) | async-done | bytes 262160 | tf_op jit(solution)/shard_map/psum | solution.py:47
  274.1 11.7 %cholesky.130 = f32[128,128]{1,0:T(8,128)S(1)} custom-call(f32[128,128]{1,0:T(8,128)S(1)} %cholesky.194), custom_call_target="Cholesky" | custom-call | tf_op jit(solution)/shard_map/jit(cholesky)/cholesky | solution.py:10
  285.9 9.8 %custom-call.17 = f32[1,128,128]{1,2,0:T(8,128)S(1)} custom-call(f32[1,128,128]{2,1,0:T(8,128)S(1)} %get-tuple-element.211), custom_call_target="InvertDiagBlocksLowerTriangular" | custom-call | tf_op jit(solution)/shard_map/jit(cholesky)/cholesky | solution.py:10
  296.2 11.7 %cholesky.147 = f32[128,128]{1,0:T(8,128)S(1)} custom-call(f32[128,128]{1,0:T(8,128)S(1)} %convolution_subtract_fusion.5), custom_call_target="Cholesky" | custom-call | tf_op jit(solution)/shard_map/jit(cholesky)/cholesky | solution.py:10
  310.0 4.2 while.30
  314.2 19.7 %custom-call.18 = f32[2,128,128]{1,2,0:T(8,128)S(1)} custom-call(f32[2,128,128]{2,1,0:T(8,128)S(1)} %get-tuple-element.131), custom_call_target="InvertDiagBlocksLowerTriangular" | custom-call | tf_op jit(solution)/shard_map/triangular_solve/custom-call.0 | solution.py:11
  337.2 24.6 %all_gather.7 = bf16[1024,256]{0,1:T(8,128)(2,1)S(1)} all-gather(bf16[128,256]{0,1:T(8,128)(2,1)S(1)} %fusion.31), channel_id=1, replica_groups=mesh['wide'=32,'narrow'=8] {'narrow'}, dimensions={0}, use_global_device_ids=true | all-gather | bytes 589824 | tf_op jit(solution)/shard_map/all_gather | solution.py:72
  362.9 2.4 broadcast_in_dim.14
  365.4 159.6 %while.29 = (s32[]{:T(128)}, f32[64,64,256]{2,1,0:T(8,128)}, s32[]{:T(128)}, s32[16]{0:T(128)S(1)}, bf16[16,64,4096]{1,2,0:T(8,128)(2,1)}, /*index=5*/s32[16]{0:...) while((s32[]{:T(128)}, f32[64,64,256]{2,1,0:T(8,128)}, ...), condition=%wide.region_12.16_spmd, body=%wide.region_10.15_spmd.sunk | while | flops 136331280 | bytes 2556253 | solution.py:89
  374.5 1.5 fusion.72
  385.1 1.5 fusion.72
  395.7 1.5 fusion.72
  406.3 1.5 fusion.72
  416.9 1.5 fusion.72
  427.5 1.5 fusion.72
  448.6 1.5 fusion.72
  459.2 1.5 fusion.72
  469.8 1.5 fusion.72
  480.4 1.5 fusion.72
  491.0 1.5 fusion.72
  512.2 1.5 fusion.72
  522.8 1.5 fusion.72
  525.7 89.8 %all-reduce.6.cloned.1.call-done = f32[256,256]{0,1:T(8,128)} async-done(((f32[256,256]{0,1:T(8,128)}), f32[256,256]{0,1:T(8,128)}) %all-reduce.6.cloned.1.call-update) | async-done | bytes 262160 | tf_op jit(solution)/shard_map/psum | solution.py:73
  616.7 11.7 %cholesky.164 = f32[128,128]{1,0:T(8,128)S(1)} custom-call(f32[128,128]{1,0:T(8,128)S(1)} %cholesky.197), custom_call_target="Cholesky" | custom-call | tf_op jit(solution)/shard_map/jit(cholesky)/cholesky | solution.py:10
  628.5 9.8 %custom-call.20 = f32[1,128,128]{1,2,0:T(8,128)S(1)} custom-call(f32[1,128,128]{2,1,0:T(8,128)S(1)} %get-tuple-element.207), custom_call_target="InvertDiagBlocksLowerTriangular" | custom-call | tf_op jit(solution)/shard_map/jit(cholesky)/cholesky | solution.py:10
  638.7 11.7 %cholesky.181 = f32[128,128]{1,0:T(8,128)S(1)} custom-call(f32[128,128]{1,0:T(8,128)S(1)} %convolution_subtract_fusion.2), custom_call_target="Cholesky" | custom-call | tf_op jit(solution)/shard_map/jit(cholesky)/cholesky | solution.py:10
  653.1 4.1 while.31
  657.3 19.7 %custom-call.21 = f32[2,128,128]{1,2,0:T(8,128)S(1)} custom-call(f32[2,128,128]{2,1,0:T(8,128)S(1)} %get-tuple-element.133), custom_call_target="InvertDiagBlocksLowerTriangular" | custom-call | tf_op jit(solution)/shard_map/triangular_solve/custom-call.0 | solution.py:11
  (279 shorter events, 154.6 us)
Async XLA Ops:
  8.0 54.6 %all-gather.2.cloned.1.call-start = ((), (), s32[]{:S(2)}) async-start(), calls=%async_computation.3 | async-start | bytes 2162688 | tf_op jit(solution)/shard_map/all_gather | solution.py:48
  8.7 263.9 %all-reduce.4.cloned.1.call-start = ((), (), s32[]{:S(2)}) async-start(), calls=%async_computation.2 | async-start | bytes 524288 | tf_op jit(solution)/shard_map/psum | solution.py:47
  10.7 323.2 %reduce-scatter.3.cloned.1.call-start = ((), (), s32[]{:S(2)}) async-start(), calls=%async_computation.4 | async-start | bytes 1179648 | tf_op jit(solution)/shard_map/reduce_scatter | solution.py:67
  10.7 15.7 %copy-start.2 = (s32[1,1,16]{2,1,0:T(1,128)S(1)}, s32[1,1,16]{2,1,0:T(1,128)}, u32[]{:S(2)}) copy-start(s32[1,1,16]{2,1,0:T(1,128)} %param.18) | copy-start | bytes 196
  10.7 51.9 %copy-start.1 = (bf16[1024,256]{1,0:T(8,128)(2,1)S(1)}, bf16[1024,256]{1,0:T(8,128)(2,1)}, u32[]{:S(2)}) copy-start(bf16[1024,256]{1,0:T(8,128)(2,1)} %param.22) | copy-start | bytes 1572868
  10.7 51.9 %copy-start.3 = (s32[1,1,16]{2,1,0:T(1,128)S(1)}, s32[1,1,16]{2,1,0:T(1,128)}, u32[]{:S(2)}) copy-start(s32[1,1,16]{2,1,0:T(1,128)} %param.17) | copy-start | bytes 196
  10.7 51.9 %copy-start.4 = (s32[1,1,16]{2,1,0:T(1,128)S(1)}, s32[1,1,16]{2,1,0:T(1,128)}, u32[]{:S(2)}) copy-start(s32[1,1,16]{2,1,0:T(1,128)} %param.19) | copy-start | bytes 196
  206.9 1.0 copy-start
  207.9 407.6 %all-reduce.6.cloned.1.call-start = ((), (), s32[]{:S(2)}) async-start(), calls=%async_computation.5 | async-start | bytes 524288 | tf_op jit(solution)/shard_map/psum | solution.py:73
  362.9 314.1 %reduce-scatter.5.cloned.1.call-start = ((), (), s32[]{:S(2)}) async-start(), calls=%async_computation.6 | async-start | bytes 4325376 | tf_op jit(solution)/shard_map/reduce_scatter | solution.py:92
Sparse Core Ops, SparseCore 0:
  11.4 51.1 all-gather.1
  208.0 42.8 reduce-scatter.2
  525.1 93.6 reduce-scatter.4
Sparse Core Ops, SparseCore 1:
  14.7 257.9 all-reduce.3
  363.0 252.5 all-reduce.5
where the time goes:
time: 694 us; the launch traced here: 688 us
  waiting for transfers between devices  191 us (28%)
  loops' own time  155 us (22%)
  other arithmetic  143 us (21%)
  local copies, waits for them, and re-layouts  121 us (17%)
  matrix products  34.1 us (5%)
  blocking collectives  24.6 us (4%)
  between operations  18.1 us (3%)
    psum x1, waiting for transfers between devices, local(): gram_a = lax.psum(column_gram(a_half), ('wide', 'narrow'))  89.8 us
    another operation x1, loops' own time, local(): lax.fori_loop(0, live_count, second_step, jnp.zeros((width_slots, tile_ro...  79.1 us
    another operation x1, loops' own time, local(): lax.fori_loop(0, live_count, first_step, jnp.zeros((narrow_count * TI_DEV...  75.7 us
    another operation x13, other arithmetic, right_solve(): chol_lower = jnp.linalg.cholesky(matrix)  68.6 us
    psum x1, waiting for transfers between devices, local(): gram_b = lax.psum(column_gram(factor_b), ('wide', 'narrow'))  64.7 us
    another operation x5, other arithmetic, right_solve(): lax.linalg.triangular_solve(chol_lower, target, left_side=False, lower=Tr...  39.4 us
    all_gather x1, waiting for transfers between devices, local(): gathered = lax.all_gather(factor_b, 'wide', axis=0, tiled=True)  36.2 us
    all_gather x1, blocking collectives, local(): a_rows = lax.all_gather(a_half, 'narrow', axis=0, tiled=True)  24.6 us
  transfers between devices with their start and end apart: 5, of which 3 were waited for; matrix products, arithmetic and copies ran while one was open for 42% of the time, Pallas kernels for 0%

commit v1 on v0

--- a/solution.py
+++ b/solution.py
@@ -44,7 +44,7 @@
     owners = second_ids // second_local
     inside = second_ids % second_local
     gram_c = column_gram(factor_c)
-    gram_b = lax.psum(column_gram(factor_b), ("wide", "narrow"))
+    gram_b = lax.psum(lax.psum(column_gram(factor_b), "wide"), "narrow")
     gathered = lax.all_gather(factor_b, "wide", axis=0, tiled=True)
     b_tiles = gathered.reshape(wide_count * second_local, tile_rows, rank_width)
     b_pick = owners * second_local + inside

time: 694 us -> 780 us (1.12)
  waiting for transfers between devices: 191 us -> 279 us
    psum x1 -> x2, waiting for transfers between devices: 64.7 us -> 100 us  [local(): gram_b = lax.psum(lax.psum(column_gram(factor_b), 'wide'), 'narrow')]
    reduce_scatter x1, waiting for transfers between devices: 0.02 us -> 31.1 us  [local(): lax.psum_scatter(second_part.reshape(-1, rank_width), 'wide', scatter_dim...]
    all_gather x1, waiting for transfers between devices: 36.2 us -> 51 us  [local(): gathered = lax.all_gather(factor_b, 'wide', axis=0, tiled=True)]
  transfers between devices with their start and end apart: 5 -> 6, of which waited for: 3 -> 4; matrix products, arithmetic and copies ran while one was open for 42% -> 37% of each run, Pallas kernels for 0% -> 0%
where the time goes in v1:
time: 780 us; the launch traced here: 773 us
  waiting for transfers between devices  279 us (36%)
  loops' own time  155 us (20%)
  other arithmetic  143 us (18%)
  local copies, waits for them, and re-layouts  121 us (16%)
  matrix products  34.1 us (4%)
  blocking collectives  23.3 us (3%)
  between operations  17 us (2%)
    psum x2, waiting for transfers between devices, local(): gram_b = lax.psum(lax.psum(column_gram(factor_b), 'wide'), 'narrow')  100 us
    psum x1, waiting for transfers between devices, local(): gram_a = lax.psum(column_gram(a_half), ('wide', 'narrow'))  95.6 us
    another operation x1, loops' own time, local(): lax.fori_loop(0, live_count, second_step, jnp.zeros((width_slots, tile_ro...  79.1 us
    another operation x1, loops' own time, local(): lax.fori_loop(0, live_count, first_step, jnp.zeros((narrow_count * TI_DEV...  75.7 us
    another operation x13, other arithmetic, right_solve(): chol_lower = jnp.linalg.cholesky(matrix)  68.6 us
    all_gather x1, waiting for transfers between devices, local(): gathered = lax.all_gather(factor_b, 'wide', axis=0, tiled=True)  51 us
    another operation x5, other arithmetic, right_solve(): lax.linalg.triangular_solve(chol_lower, target, left_side=False, lower=Tr...  39.4 us
    reduce_scatter x1, waiting for transfers between devices, local(): lax.psum_scatter(second_part.reshape(-1, rank_width), 'wide', scatter_dim...  31.1 us
  transfers between devices with their start and end apart: 6, of which 4 were waited for; matrix products, arithmetic and copies ran while one was open for 37% of the time, Pallas kernels for 0%

profile of v1, /device:TPU:2, one launch (start us, length us, event | category | flops | bytes accessed | tf_op | source)
XLA Modules:
  0.0 773.4 jit_solution(11975603047328542560)
XLA Ops:
  7.2 1.8 fusion.35
  9.9 15.6 %copy.22 = bf16[1,1,16,64,4096]{3,4,2,1,0:T(8,128)(2,1)} copy(bf16[1,1,16,64,4096]{4,3,2,1,0:T(8,128)(2,1)} %param.16) | data formatting | bytes 16777216 | tf_op args[0]
  25.6 100.4 %all-reduce.5.cloned.1.call-done = f32[256,256]{0,1:T(8,128)} async-done(((f32[256,256]{0,1:T(8,128)}), f32[256,256]{0,1:T(8,128)}) %all-reduce.5.cloned.1.call-update) | async-done | bytes 262160 | tf_op jit(solution)/shard_map/psum | solution.py:47
  126.1 51.0 %all-gather.2.cloned.1.call-done = bf16[4096,256]{1,0:T(8,128)(2,1)} async-done(((bf16[128,256]{1,0:T(8,128)(2,1)}), bf16[4096,256]{1,0:T(8,128)(2,1)}) %all-gather.2.cloned.1.call-update) | async-done | bytes 2097168 | tf_op jit(solution)/shard_map/all_gather | solution.py:48
  177.3 144.1 %while.28 = (s32[]{:T(128)}, f32[16,64,256]{2,1,0:T(8,128)S(1)}, s32[]{:T(128)}, s32[16]{0:T(128)S(1)}, bf16[16,64,4096]{1,2,0:T(8,128)(2,1)}, /*index=5*/s32[16...) while((s32[]{:T(128)}, f32[16,64,256]{2,1,0:T(8,128)S(1)}, ...), condition=%wide.region_8.10_spmd, body=%wide.region_6.9_spmd.sunk | while | flops 136331280 | bytes 2556253 | solution.py:61
  324.0 11.7 %cholesky.130 = f32[128,128]{1,0:T(8,128)S(1)} custom-call(f32[128,128]{1,0:T(8,128)S(1)} %cholesky.194), custom_call_target="Cholesky" | custom-call | tf_op jit(solution)/shard_map/jit(cholesky)/cholesky | solution.py:10
  335.7 9.8 %custom-call.17 = f32[1,128,128]{1,2,0:T(8,128)S(1)} custom-call(f32[1,128,128]{2,1,0:T(8,128)S(1)} %get-tuple-element.211), custom_call_target="InvertDiagBlocksLowerTriangular" | custom-call | tf_op jit(solution)/shard_map/jit(cholesky)/cholesky | solution.py:10
  346.0 11.7 %cholesky.147 = f32[128,128]{1,0:T(8,128)S(1)} custom-call(f32[128,128]{1,0:T(8,128)S(1)} %convolution_subtract_fusion.5), custom_call_target="Cholesky" | custom-call | tf_op jit(solution)/shard_map/jit(cholesky)/cholesky | solution.py:10
  359.9 4.2 while.30
  364.0 19.7 %custom-call.18 = f32[2,128,128]{1,2,0:T(8,128)S(1)} custom-call(f32[2,128,128]{2,1,0:T(8,128)S(1)} %get-tuple-element.131), custom_call_target="InvertDiagBlocksLowerTriangular" | custom-call | tf_op jit(solution)/shard_map/triangular_solve/custom-call.0 | solution.py:11
  387.0 23.3 %all_gather.7 = bf16[1024,256]{0,1:T(8,128)(2,1)S(1)} all-gather(bf16[128,256]{0,1:T(8,128)(2,1)S(1)} %fusion.31), channel_id=1, replica_groups=mesh['wide'=32,'narrow'=8] {'narrow'}, dimensions={0}, use_global_device_ids=true | all-gather | bytes 589824 | tf_op jit(solution)/shard_map/all_gather | solution.py:72
  411.5 2.4 broadcast_in_dim.14
  414.0 159.6 %while.29 = (s32[]{:T(128)}, f32[64,64,256]{2,1,0:T(8,128)}, s32[]{:T(128)}, s32[16]{0:T(128)S(1)}, bf16[16,64,4096]{1,2,0:T(8,128)(2,1)}, /*index=5*/s32[16]{0:...) while((s32[]{:T(128)}, f32[64,64,256]{2,1,0:T(8,128)}, ...), condition=%wide.region_13.17_spmd, body=%wide.region_11.16_spmd.sunk | while | flops 136331280 | bytes 2556253 | solution.py:89
  423.1 1.5 fusion.72
  433.7 1.5 fusion.72
  444.3 1.5 fusion.72
  454.9 1.5 fusion.72
  465.5 1.5 fusion.72
  476.1 1.5 fusion.72
  497.2 1.5 fusion.72
  507.8 1.5 fusion.72
  518.4 1.5 fusion.72
  529.0 1.5 fusion.72
  539.6 1.5 fusion.72
  571.4 1.5 fusion.72
  574.3 95.6 %all-reduce.9.cloned.1.call-done = f32[256,256]{0,1:T(8,128)} async-done(((f32[256,256]{0,1:T(8,128)}), f32[256,256]{0,1:T(8,128)}) %all-reduce.9.cloned.1.call-update) | async-done | bytes 262160 | tf_op jit(solution)/shard_map/psum | solution.py:73
  671.2 11.7 %cholesky.164 = f32[128,128]{1,0:T(8,128)S(1)} custom-call(f32[128,128]{1,0:T(8,128)S(1)} %cholesky.197), custom_call_target="Cholesky" | custom-call | tf_op jit(solution)/shard_map/jit(cholesky)/cholesky | solution.py:10
  682.9 9.8 %custom-call.20 = f32[1,128,128]{1,2,0:T(8,128)S(1)} custom-call(f32[1,128,128]{2,1,0:T(8,128)S(1)} %get-tuple-element.207), custom_call_target="InvertDiagBlocksLowerTriangular" | custom-call | tf_op jit(solution)/shard_map/jit(cholesky)/cholesky | solution.py:10
  693.2 11.7 %cholesky.181 = f32[128,128]{1,0:T(8,128)S(1)} custom-call(f32[128,128]{1,0:T(8,128)S(1)} %convolution_subtract_fusion.2), custom_call_target="Cholesky" | custom-call | tf_op jit(solution)/shard_map/jit(cholesky)/cholesky | solution.py:10
  707.6 4.1 while.31
  711.7 19.7 %custom-call.21 = f32[2,128,128]{1,2,0:T(8,128)S(1)} custom-call(f32[2,128,128]{2,1,0:T(8,128)S(1)} %get-tuple-element.133), custom_call_target="InvertDiagBlocksLowerTriangular" | custom-call | tf_op jit(solution)/shard_map/triangular_solve/custom-call.0 | solution.py:11
  731.4 31.1 %reduce-scatter.5.cloned.1.call-done = f32[128,256]{1,0:T(8,128)} async-done(((f32[4096,256]{1,0:T(8,128)}), f32[128,256]{1,0:T(8,128)}) %reduce-scatter.5.cloned.1.call-update) | async-done | bytes 131088 | tf_op jit(solution)/shard_map/reduce_scatter | solution.py:92
  (282 shorter events, 156.1 us)
Async XLA Ops:
  7.2 118.8 %all-reduce.5.cloned.1.call-start = ((), (), s32[]{:S(2)}) async-start(), calls=%async_computation.2 | async-start | bytes 524288 | tf_op jit(solution)/shard_map/psum | solution.py:47
  9.1 168.0 %all-gather.2.cloned.1.call-start = ((), (), s32[]{:S(2)}) async-start(), calls=%async_computation.4 | async-start | bytes 2162688 | tf_op jit(solution)/shard_map/all_gather | solution.py:48
  9.8 312.6 %all-reduce.7.cloned.1.call-start = ((), (), s32[]{:S(2)}) async-start(), calls=%async_computation.3 | async-start | bytes 524288 | tf_op jit(solution)/shard_map/psum | solution.py:47
  9.9 15.7 %copy-start.2 = (s32[1,1,16]{2,1,0:T(1,128)S(1)}, s32[1,1,16]{2,1,0:T(1,128)}, u32[]{:S(2)}) copy-start(s32[1,1,16]{2,1,0:T(1,128)} %param.18) | copy-start | bytes 196
  9.9 167.3 %copy-start.1 = (bf16[1024,256]{1,0:T(8,128)(2,1)S(1)}, bf16[1024,256]{1,0:T(8,128)(2,1)}, u32[]{:S(2)}) copy-start(bf16[1024,256]{1,0:T(8,128)(2,1)} %param.22) | copy-start | bytes 1572868
  9.9 167.3 %copy-start.3 = (s32[1,1,16]{2,1,0:T(1,128)S(1)}, s32[1,1,16]{2,1,0:T(1,128)}, u32[]{:S(2)}) copy-start(s32[1,1,16]{2,1,0:T(1,128)} %param.17) | copy-start | bytes 196
  9.9 167.3 %copy-start.4 = (s32[1,1,16]{2,1,0:T(1,128)S(1)}, s32[1,1,16]{2,1,0:T(1,128)}, u32[]{:S(2)}) copy-start(s32[1,1,16]{2,1,0:T(1,128)} %param.19) | copy-start | bytes 196
  126.0 257.7 %reduce-scatter.3.cloned.1.call-start = ((), (), s32[]{:S(2)}) async-start(), calls=%async_computation.5 | async-start | bytes 1179648 | tf_op jit(solution)/shard_map/reduce_scatter | solution.py:67
  321.4 1.0 copy-start
  322.4 347.6 %all-reduce.9.cloned.1.call-start = ((), (), s32[]{:S(2)}) async-start(), calls=%async_computation.6 | async-start | bytes 524288 | tf_op jit(solution)/shard_map/psum | solution.py:73
  411.5 351.1 %reduce-scatter.5.cloned.1.call-start = ((), (), s32[]{:S(2)}) async-start(), calls=%async_computation.7 | async-start | bytes 4325376 | tf_op jit(solution)/shard_map/reduce_scatter | solution.py:92
Sparse Core Ops, SparseCore 0:
  11.2 114.7 all-reduce.4
  128.6 48.5 all-gather.1
  179.4 72.7 all-reduce.6
  322.5 42.6 reduce-scatter.2
  411.6 258.3 all-reduce.8
  673.8 88.7 reduce-scatter.4
